TPU v7x, 32 devices: a whole 2x2x4 slice. The times are simulated.
32 devices in a mesh: gx: 16 (over z, x, core), gy: 2 (over y).
Axes of the slice: x: 2, y: 2, z: 4, core: 2. Of those that a mesh axis runs over, the one named last changes fastest.
Arguments:
- temp_old: float32 [256, 64, 1024], P('gx', 'gy'), may hold values from -6 to 6
- capacity: float32 [256, 64, 1024], P('gx', 'gy'), may hold values from 0.05 to 0.5
- soil_class: int32 [256, 64, 1024], P('gx', 'gy'), may hold values from 0 to 7
- cond_table: float32 [8], replicated, may hold values from 0.3 to 3
- losses: float32 [8192, 128], P(('gx', 'gy')), may hold values from 0.1 to 10
- owner: int32 [8192, 1], P(('gx', 'gy')), may hold values from 0 to 1; in each aligned block of 256 rows (0 to 255, 256 to 511, ...) at most 256 rows name the same one
- column: int32 [8192], P(('gx', 'gy')), may hold values from 0 to 511
- injection: float32 [128, 1024], replicated, may hold values from -0.5 to 0.5
Outputs:
- temp_new: float32 [256, 64, 1024], P('gx', 'gy')
Inputs may be any that keep to these rules, and one draw needn't show every extreme that they name: In each device's block of 256 rows no owner is named by more than 256 rows, a bound that some block reaches.
All inputs are finite; a program needn't handle non-finite values.
Results may differ from a plain program's by a relative error of at most 0.000061.
Values sent between devices are 32-bit elements; how exact they have to be, the bound alone decides.
A program may use at most 64 MiB of HBM per device.

v0:
```python
import jax
import jax.numpy as jnp
from jax import lax
from jax.sharding import PartitionSpec as P

SWEEPS = 4
NCLS = 8


def extended(x, sides, width):
    for axis, dim in sides:
        count, length = (lax.axis_size(axis), x.shape[dim])
        up = [(i, (i + 1) % count) for i in range(count - 1)]
        down = [(j, i) for i, j in up]
        last = lax.slice_in_dim(x, length - width, length, axis=dim)
        first = lax.slice_in_dim(x, 0, width, axis=dim)
        before = lax.ppermute(last, axis, up)
        after = lax.ppermute(first, axis, down)
        x = jnp.concatenate([before, x, after], axis=dim)
    return x


def face_terms(cond_pad):
    center = cond_pad[1:-1, 1:-1, 1:-1]
    return [
        0.5 * (center + cond_pad[2:, 1:-1, 1:-1]),
        0.5 * (center + cond_pad[:-2, 1:-1, 1:-1]),
        0.5 * (center + cond_pad[1:-1, 2:, 1:-1]),
        0.5 * (center + cond_pad[1:-1, :-2, 1:-1]),
        0.5 * (center + cond_pad[1:-1, 1:-1, 2:]),
        0.5 * (center + cond_pad[1:-1, 1:-1, :-2]),
    ]


def neighbour_sum(faces, temp_pad):
    total = faces[0] * temp_pad[2:, 1:-1, 1:-1] + faces[1] * temp_pad[:-2, 1:-1, 1:-1]
    total = total + faces[2] * temp_pad[1:-1, 2:, 1:-1] + faces[3] * temp_pad[1:-1, :-2, 1:-1]
    total = total + faces[4] * temp_pad[1:-1, 1:-1, 2:] + faces[5] * temp_pad[1:-1, 1:-1, :-2]
    return total


def depth_pad(field):
    return jnp.pad(field, ((0, 0), (0, 0), (1, 1)))


def shards(temp_old, capacity, soil_class, cond_table, losses, owner, column, injection):
    cx, cy, nz = temp_old.shape
    cond = jnp.zeros(temp_old.shape, jnp.float32)
    for klass in range(NCLS):
        cond = cond + jnp.where(soil_class == klass, cond_table[klass], jnp.float32(0.0))
    cond_pad = depth_pad(extended(cond, (("gx", 0), ("gy", 1)), 1))
    faces = face_terms(cond_pad)
    diag = capacity + faces[0] + faces[1] + faces[2] + faces[3] + faces[4] + faces[5]
    my_slab = lax.axis_index("gy")
    recv_loss, recv_owner, recv_col = (
        lax.all_gather(losses, "gy", axis=0, tiled=True),
        lax.all_gather(owner, "gy", axis=0, tiled=True),
        lax.all_gather(column, "gy", axis=0, tiled=True),
    )
    cols = jnp.where(recv_owner[:, 0] == my_slab, recv_col, -1)
    profile = jnp.dot(
        recv_loss, injection, precision=lax.Precision.HIGHEST, preferred_element_type=jnp.float32
    )
    picker = (cols[None, :] == jnp.arange(cx * cy, dtype=jnp.int32)[:, None]).astype(jnp.float32)
    source = jnp.dot(
        picker, profile, precision=lax.Precision.HIGHEST, preferred_element_type=jnp.float32
    )
    rhs = capacity * temp_old + source.reshape(cx, cy, nz)
    temp = temp_old
    for sweep in range(SWEEPS):
        temp_pad = depth_pad(extended(temp, (("gx", 0), ("gy", 1)), 1))
        nbsum = neighbour_sum(faces, temp_pad)
        temp = temp + 0.8 * (rhs - diag * temp + nbsum) / diag
    return temp


def solution(mesh):
    return jax.shard_map(
        shards,
        mesh=mesh,
        in_specs=(
            P("gx", "gy", None),
            P("gx", "gy", None),
            P("gx", "gy", None),
            P(),
            P(("gx", "gy"), None),
            P(("gx", "gy"), None),
            P(("gx", "gy")),
            P(),
        ),
        out_specs=P("gx", "gy", None),
        check_vma=False,
    )
```

profile of v0, /device:TPU:9, one launch (start us, length us, event | category | flops | bytes accessed | tf_op | source)
XLA Modules:
  0.0 173.9 jit_solution(16806642427214263519)
XLA Ops:
  0.0 1.7 fusion.70
  1.7 2.6 %collective-permute-start.4 = (f32[1,32,1024]{2,1,0:T(8,128)S(1)}, f32[1,32,1024]{2,1,0:T(8,128)S(1)}, u32[]{:S(2)}, u32[]{:S(2)}) collective-permute-start(f32[1,32,1024]{2,1,0:T(8,128)S(1)} %get-tuple-element.23), channel_id=1, source_target_pairs={{2,0},{4,2},{6,4},{8,6},{10,8},{12,10},{14,12},{16,14},{18,16},{20... | collective-permute-start | bytes 393224 | tf_op jit(solution)/shard_map/ppermute | solution.py:18
  4.3 3.0 %collective-permute-start.5 = (f32[1,32,1024]{2,1,0:T(8,128)}, f32[1,32,1024]{2,1,0:T(8,128)S(1)}, u32[]{:S(2)}, u32[]{:S(2)}) collective-permute-start(f32[1,32,1024]{2,1,0:T(8,128)} %get-tuple-element.24), channel_id=1, source_target_pairs={{0,2},{2,4},{4,6},{6,8},{8,10},{10,12},{12,14},{14,16},{16,18},{18... | collective-permute-start | bytes 393224 | tf_op jit(solution)/shard_map/ppermute | solution.py:17
  7.3 1.6 fusion.71
  8.9 8.1 %select_add_fusion = f32[16,32,1024]{2,1,0:T(8,128)S(1)} fusion(s32[16,32,1024]{2,1,0:T(8,128)} %param.10, f32[]{:T(128)} %bitcast.10, f32[]{:T(128)} %bitcast.9, f32[]{:T(128)} %bitcast.8, f32[]{:T(128)} %bitcast.7, f32[]{:T(128)} %bitcast.6, f32[]{:T(128)} %bitcast.5, f32[]{:T(128)} %bitcast.4, f32[]{:T(128)} %bitcast.3), kind=kLoop, calls=%fused_computation.130 | loop fusion | flops 12058624 | bytes 4194336 | tf_op jit(solution)/shard_map/add | solution.py:50
  17.1 0.7 fusion.69
  17.7 2.4 %collective-permute-start.1 = (f32[1,32,1024]{2,1,0:T(8,128)}, f32[1,32,1024]{2,1,0:T(8,128)S(1)}, u32[]{:S(2)}, u32[]{:S(2)}) collective-permute-start(f32[1,32,1024]{2,1,0:T(8,128)} %get-tuple-element.21), channel_id=1, source_target_pairs={{0,2},{2,4},{4,6},{6,8},{8,10},{10,12},{12,14},{14,16},{16,18},{18... | collective-permute-start | bytes 393224 | tf_op jit(solution)/shard_map/ppermute | solution.py:17
  20.1 1.9 %collective-permute-start = (f32[1,32,1024]{2,1,0:T(8,128)S(1)}, f32[1,32,1024]{2,1,0:T(8,128)S(1)}, u32[]{:S(2)}, u32[]{:S(2)}) collective-permute-start(f32[1,32,1024]{2,1,0:T(8,128)S(1)} %get-tuple-element.22), channel_id=1, source_target_pairs={{2,0},{4,2},{6,4},{8,6},{10,8},{12,10},{14,12},{16,14},{18,16},{20... | collective-permute-start | bytes 393224 | tf_op jit(solution)/shard_map/ppermute | solution.py:18
  22.1 3.1 %all_gather.9 = s32[512,1]{0,1:T(1,128)S(1)} all-gather(s32[256,1]{0,1:T(1,128)S(1)} %copy-done.7), channel_id=1, replica_groups=mesh['gx'=16,'gy'=2] {'gy'}, dimensions={0}, use_global_device_ids=true | all-gather | bytes 3072 | tf_op jit(solution)/shard_map/all_gather | solution.py:57
  25.2 3.1 %all-gather = s32[2,1,256]{2,1,0:T(1,128)S(1)} all-gather(s32[1,1,256]{2,1,0:T(1,128)S(1)} %bitcast.19), channel_id=1, replica_groups=mesh['gx'=16,'gy'=2] {'gy'}, dimensions={0}, use_global_device_ids=true | all-gather | bytes 3072 | tf_op jit(solution)/shard_map/all_gather | solution.py:58
  28.2 4.5 %all_gather.11 = f32[512,128]{1,0:T(8,128)S(1)} all-gather(f32[256,128]{1,0:T(8,128)S(1)} %copy-done.6), channel_id=1, replica_groups=mesh['gx'=16,'gy'=2] {'gy'}, dimensions={0}, use_global_device_ids=true | all-gather | bytes 393216 | tf_op jit(solution)/shard_map/all_gather | solution.py:56
  32.8 1.8 %fusion.72 = f32[512,1024]{1,0:T(8,128)S(1)} fusion(f32[512,128]{1,0:T(8,128)S(1)} %all_gather.11, f32[128,1024]{1,0:T(8,128)S(1)} %copy-done), kind=kOutput, calls=%fused_computation.159 | convolution fusion | flops 805306368 | bytes 2883584 | tf_op jit(solution)/shard_map/dot_general | solution.py:61
  34.6 2.0 %fusion.63 = f32[512,1024]{1,0:T(8,128)S(1)} fusion(f32[512,1024]{1,0:T(8,128)S(1)} %fusion.72, s32[512]{0:T(512)S(1)} %broadcast_select_fusion), kind=kOutput, calls=%fused_computation.133 | convolution fusion | flops 3221487616 | bytes 4196352 | tf_op jit(solution)/shard_map/dot_general | solution.py:65
  36.6 0.1 constant_dynamic-update-slice_fusion.1
  36.8 0.1 fusion.65
  37.0 1.3 collective-permute-start.6
  38.3 4.0 %collective-permute-start.7 = (f32[18,1,1024]{2,0,1:T(8,128)S(1)}, f32[18,1,1024]{2,0,1:T(8,128)S(1)}, u32[]{:S(2)}, u32[]{:S(2)}) collective-permute-start(f32[18,1,1024]{2,0,1:T(8,128)S(1)} %copy.37), channel_id=1, source_target_pairs={{0,1},{2,3},{4,5},{6,7},{8,9},{10,11},{12,13},{14,15},{16,17},{18,... | collective-permute-start | bytes 221192 | tf_op jit(solution)/shard_map/ppermute | solution.py:17
  42.3 0.1 pad_maximum_fusion.45
  42.5 1.3 collective-permute-start.2
  43.8 4.2 %collective-permute-start.3 = (f32[18,1,1024]{2,0,1:T(8,128)S(1)}, f32[18,1,1024]{2,0,1:T(8,128)S(1)}, u32[]{:S(2)}, u32[]{:S(2)}) collective-permute-start(f32[18,1,1024]{2,0,1:T(8,128)S(1)} %copy.31), channel_id=1, source_target_pairs={{0,1},{2,3},{4,5},{6,7},{8,9},{10,11},{12,13},{14,15},{16,17},{18,... | collective-permute-start | bytes 221192 | tf_op jit(solution)/shard_map/ppermute | solution.py:17
  48.0 0.1 copy.36
  48.1 0.1 copy.38
  48.1 3.3 %select_maximum_fusion.12 = f32[18,34,1026]{2,1,0:T(8,128)} fusion(f32[18,1,1024]{2,1,0:T(1,128)S(1)} %copy.36, f32[18,32,1024]{2,1,0:T(8,128)S(1)} %constant_dynamic-update-slice_fusion, f32[18,1,1024]{2,1,0:T(1,128)S(1)} %copy.38), kind=kLoop, calls=%fused_computation.14 | loop fusion | flops 5023296 | bytes 5018400 | tf_op jit(solution)/shard_map/concatenate | solution.py:19
  51.4 0.1 copy.30
  51.5 0.1 copy.32
  51.6 3.2 %select_maximum_fusion.14 = f32[18,34,1026]{2,1,0:T(8,128)S(1)} fusion(f32[18,1,1024]{2,1,0:T(1,128)S(1)} %copy.30, f32[18,1,1024]{2,1,0:T(1,128)S(1)} %copy.32, f32[1,32,1024]{2,1,0:T(8,128)S(1)} %collective-permute-done, f32[16,32,1024]{2,1,0:T(8,128)S(1)} %select_add_fusion, f32[1,32,1024]{2,1,0:T(8,128)S(1)} %collective-permute-done.1), kind=kLoop, calls=%fused_computation.16 | loop fusion | flops 7534944 | bytes 5018400 | tf_op jit(solution)/shard_map/concatenate | solution.py:19
  54.8 9.9 %fusion.44 = f32[16,32,1024]{2,1,0:T(8,128)S(1)} fusion(f32[16,32,1024]{2,1,0:T(8,128)S(1)} %copy-done.1, f32[18,34,1026]{2,1,0:T(8,128)} %select_maximum_fusion.12, f32[18,32,1024]{2,1,0:T(8,128)} %copy-done.5, f32[18,1,1024]{2,1,0:T(1,128)S(1)} %copy.38, f32[18,1,1024]{2,1,0:T(1,128)S(1)} %copy.36, f32[1,32,1024]{2,1,0:T(8,128)S(1)} %collective-permute-done.5, ...), kind=kLoop, calls=%fused_computation.95 | loop fusion | flops 25690112 | bytes 22052864 | tf_op jit(solution)/shard_map/add | solution.py:73
  64.7 8.4 %collective-permute-start.9 = (f32[1,32,1024]{2,1,0:T(8,128)S(1)}, f32[1,32,1024]{2,1,0:T(8,128)S(1)}, u32[]{:S(2)}, u32[]{:S(2)}) collective-permute-start(f32[1,32,1024]{2,1,0:T(8,128)S(1)} %get-tuple-element.19), channel_id=1, source_target_pairs={{0,2},{2,4},{4,6},{6,8},{8,10},{10,12},{12,14},{14,16},{16,18},{18... | collective-permute-start | bytes 393224 | tf_op jit(solution)/shard_map/ppermute | solution.py:17
  73.2 1.9 %collective-permute-start.8 = (f32[1,32,1024]{2,1,0:T(8,128)S(1)}, f32[1,32,1024]{2,1,0:T(8,128)S(1)}, u32[]{:S(2)}, u32[]{:S(2)}) collective-permute-start(f32[1,32,1024]{2,1,0:T(8,128)S(1)} %get-tuple-element.20), channel_id=1, source_target_pairs={{2,0},{4,2},{6,4},{8,6},{10,8},{12,10},{14,12},{16,14},{18,16},{20... | collective-permute-start | bytes 393224 | tf_op jit(solution)/shard_map/ppermute | solution.py:18
  75.1 4.3 %collective-permute-done.8 = f32[1,32,1024]{2,1,0:T(8,128)S(1)} collective-permute-done((f32[1,32,1024]{2,1,0:T(8,128)S(1)}, f32[1,32,1024]{2,1,0:T(8,128)S(1)}, u32[]{:S(2)}, u32[]{:S(2)}) %collective-permute-start.8) | collective-permute-done | bytes 131104 | tf_op jit(solution)/shard_map/ppermute | solution.py:18
  79.5 0.1 pad_maximum_fusion.42
  79.6 1.3 collective-permute-start.10
  80.9 4.0 %collective-permute-start.11 = (f32[18,1,1024]{2,0,1:T(8,128)S(1)}, f32[18,1,1024]{2,0,1:T(8,128)S(1)}, u32[]{:S(2)}, u32[]{:S(2)}) collective-permute-start(f32[18,1,1024]{2,0,1:T(8,128)S(1)} %copy.43), channel_id=1, source_target_pairs={{0,1},{2,3},{4,5},{6,7},{8,9},{10,11},{12,13},{14,15},{16,17},{18,... | collective-permute-start | bytes 221192 | tf_op jit(solution)/shard_map/ppermute | solution.py:17
  84.9 0.0 collective-permute-done.10
  85.0 0.1 copy.42
  85.1 1.5 collective-permute-done.11
  86.6 0.1 copy.44
  86.6 4.4 %select_maximum_fusion.8 = f32[18,34,1026]{2,1,0:T(8,128)} fusion(f32[18,1,1024]{2,1,0:T(1,128)S(1)} %copy.42, f32[18,1,1024]{2,1,0:T(1,128)S(1)} %copy.44, f32[1,32,1024]{2,1,0:T(8,128)S(1)} %collective-permute-done.8, f32[16,32,1024]{2,1,0:T(8,128)S(1)} %fusion.44, f32[1,32,1024]{2,1,0:T(8,128)S(1)} %collective-permute-done.9), kind=kLoop, calls=%fused_computation.10 | loop fusion | flops 7534944 | bytes 5018400 | tf_op jit(solution)/shard_map/concatenate | solution.py:19
  91.0 12.0 %fusion.31 = f32[16,32,1024]{2,1,0:T(8,128)} fusion(f32[16,32,1024]{2,1,0:T(8,128)} %copy-done.3, f32[18,34,1026]{2,1,0:T(8,128)} %select_maximum_fusion.8, f32[18,1,1024]{2,1,0:T(1,128)S(1)} %copy.44, f32[1,32,1024]{2,1,0:T(8,128)S(1)} %collective-permute-done.8, f32[1,32,1024]{2,1,0:T(8,128)S(1)} %collective-permute-done.9, f32[18,1,1024]{2,1,0:T(1,128)S(1)} %copy.42, ...), kind=kLoop, calls=%fused_computation.72 | loop fusion | flops 27787264 | bytes 21790720 | tf_op jit(solution)/shard_map/add | solution.py:73
  103.0 1.1 fusion.67
  104.2 2.9 %collective-permute-start.13 = (f32[1,32,1024]{2,1,0:T(8,128)S(1)}, f32[1,32,1024]{2,1,0:T(8,128)S(1)}, u32[]{:S(2)}, u32[]{:S(2)}) collective-permute-start(f32[1,32,1024]{2,1,0:T(8,128)S(1)} %get-tuple-element.17), channel_id=1, source_target_pairs={{0,2},{2,4},{4,6},{6,8},{8,10},{10,12},{12,14},{14,16},{16,18},{18... | collective-permute-start | bytes 393224 | tf_op jit(solution)/shard_map/ppermute | solution.py:17
  107.1 2.7 %collective-permute-start.12 = (f32[1,32,1024]{2,1,0:T(8,128)S(1)}, f32[1,32,1024]{2,1,0:T(8,128)S(1)}, u32[]{:S(2)}, u32[]{:S(2)}) collective-permute-start(f32[1,32,1024]{2,1,0:T(8,128)S(1)} %get-tuple-element.18), channel_id=1, source_target_pairs={{2,0},{4,2},{6,4},{8,6},{10,8},{12,10},{14,12},{16,14},{18,16},{20... | collective-permute-start | bytes 393224 | tf_op jit(solution)/shard_map/ppermute | solution.py:18
  109.8 4.4 %collective-permute-done.12 = f32[1,32,1024]{2,1,0:T(8,128)S(1)} collective-permute-done((f32[1,32,1024]{2,1,0:T(8,128)S(1)}, f32[1,32,1024]{2,1,0:T(8,128)S(1)}, u32[]{:S(2)}, u32[]{:S(2)}) %collective-permute-start.12) | collective-permute-done | bytes 131104 | tf_op jit(solution)/shard_map/ppermute | solution.py:18
  114.2 1.3 pad_maximum_fusion.39
  115.5 1.3 collective-permute-start.14
  116.9 4.2 %collective-permute-start.15 = (f32[18,1,1024]{2,0,1:T(8,128)S(1)}, f32[18,1,1024]{2,0,1:T(8,128)S(1)}, u32[]{:S(2)}, u32[]{:S(2)}) collective-permute-start(f32[18,1,1024]{2,0,1:T(8,128)S(1)} %copy.49), channel_id=1, source_target_pairs={{0,1},{2,3},{4,5},{6,7},{8,9},{10,11},{12,13},{14,15},{16,17},{18,... | collective-permute-start | bytes 221192 | tf_op jit(solution)/shard_map/ppermute | solution.py:17
  121.1 0.1 copy.48
  121.2 1.3 collective-permute-done.15
  122.5 0.1 copy.50
  122.6 4.4 %select_maximum_fusion.4 = f32[18,34,1026]{2,1,0:T(8,128)} fusion(f32[18,1,1024]{2,1,0:T(1,128)S(1)} %copy.48, f32[18,1,1024]{2,1,0:T(1,128)S(1)} %copy.50, f32[1,32,1024]{2,1,0:T(8,128)S(1)} %collective-permute-done.12, f32[16,32,1024]{2,1,0:T(8,128)S(1)} %copy-done.4, f32[1,32,1024]{2,1,0:T(8,128)S(1)} %collective-permute-done.13), kind=kLoop, calls=%fused_computation.6 | loop fusion | flops 7534944 | bytes 5018400 | tf_op jit(solution)/shard_map/concatenate | solution.py:19
  126.9 11.5 %fusion.18 = f32[16,32,1024]{2,1,0:T(8,128)} fusion(f32[16,32,1024]{2,1,0:T(8,128)} %fusion.31, f32[18,34,1026]{2,1,0:T(8,128)} %select_maximum_fusion.4, f32[18,1,1024]{2,1,0:T(1,128)S(1)} %copy.50, f32[1,32,1024]{2,1,0:T(8,128)S(1)} %collective-permute-done.12, f32[1,32,1024]{2,1,0:T(8,128)S(1)} %collective-permute-done.13, f32[18,1,1024]{2,1,0:T(1,128)S(1)} %copy.48, ...), kind=kLoop, calls=%fused_computation.49 | loop fusion | flops 27787264 | bytes 21790720 | tf_op jit(solution)/shard_map/add | solution.py:73
  138.4 1.1 fusion.66
  139.6 2.9 %collective-permute-start.17 = (f32[1,32,1024]{2,1,0:T(8,128)S(1)}, f32[1,32,1024]{2,1,0:T(8,128)S(1)}, u32[]{:S(2)}, u32[]{:S(2)}) collective-permute-start(f32[1,32,1024]{2,1,0:T(8,128)S(1)} %get-tuple-element.15), channel_id=1, source_target_pairs={{0,2},{2,4},{4,6},{6,8},{8,10},{10,12},{12,14},{14,16},{16,18},{18... | collective-permute-start | bytes 393224 | tf_op jit(solution)/shard_map/ppermute | solution.py:17
  142.5 2.8 %collective-permute-start.16 = (f32[1,32,1024]{2,1,0:T(8,128)S(1)}, f32[1,32,1024]{2,1,0:T(8,128)S(1)}, u32[]{:S(2)}, u32[]{:S(2)}) collective-permute-start(f32[1,32,1024]{2,1,0:T(8,128)S(1)} %get-tuple-element.16), channel_id=1, source_target_pairs={{2,0},{4,2},{6,4},{8,6},{10,8},{12,10},{14,12},{16,14},{18,16},{20... | collective-permute-start | bytes 393224 | tf_op jit(solution)/shard_map/ppermute | solution.py:18
  145.3 4.4 %collective-permute-done.16 = f32[1,32,1024]{2,1,0:T(8,128)S(1)} collective-permute-done((f32[1,32,1024]{2,1,0:T(8,128)S(1)}, f32[1,32,1024]{2,1,0:T(8,128)S(1)}, u32[]{:S(2)}, u32[]{:S(2)}) %collective-permute-start.16) | collective-permute-done | bytes 131104 | tf_op jit(solution)/shard_map/ppermute | solution.py:18
  149.7 1.3 pad_maximum_fusion.36
  151.1 1.3 collective-permute-start.18
  152.4 4.0 %collective-permute-start.19 = (f32[18,1,1024]{2,0,1:T(8,128)S(1)}, f32[18,1,1024]{2,0,1:T(8,128)S(1)}, u32[]{:S(2)}, u32[]{:S(2)}) collective-permute-start(f32[18,1,1024]{2,0,1:T(8,128)S(1)} %copy.55), channel_id=1, source_target_pairs={{0,1},{2,3},{4,5},{6,7},{8,9},{10,11},{12,13},{14,15},{16,17},{18,... | collective-permute-start | bytes 221192 | tf_op jit(solution)/shard_map/ppermute | solution.py:17
  156.4 0.0 collective-permute-done.18
  156.4 0.1 copy.54
  156.5 1.5 collective-permute-done.19
  158.0 0.1 copy.56
  158.1 4.4 %select_maximum_fusion = f32[18,34,1026]{2,1,0:T(8,128)} fusion(f32[18,1,1024]{2,1,0:T(1,128)S(1)} %copy.54, f32[18,1,1024]{2,1,0:T(1,128)S(1)} %copy.56, f32[1,32,1024]{2,1,0:T(8,128)S(1)} %collective-permute-done.16, f32[16,32,1024]{2,1,0:T(8,128)S(1)} %copy-done.2, f32[1,32,1024]{2,1,0:T(8,128)S(1)} %collective-permute-done.17), kind=kLoop, calls=%fused_computation.2 | loop fusion | flops 7534944 | bytes 5018400 | tf_op jit(solution)/shard_map/concatenate | solution.py:19
  162.5 11.5 %fusion.5 = f32[16,32,1024]{2,1,0:T(8,128)} fusion(f32[16,32,1024]{2,1,0:T(8,128)} %fusion.18, f32[18,34,1026]{2,1,0:T(8,128)} %select_maximum_fusion, f32[18,1,1024]{2,1,0:T(1,128)S(1)} %copy.56, f32[1,32,1024]{2,1,0:T(8,128)S(1)} %collective-permute-done.16, f32[1,32,1024]{2,1,0:T(8,128)S(1)} %collective-permute-done.17, f32[18,1,1024]{2,1,0:T(1,128)S(1)} %copy.54, ...), kind=kLoop, calls=%fused_computation.26 | loop fusion | flops 27787264 | bytes 21790720 | tf_op jit(solution)/shard_map/add | solution.py:73
  (45 shorter events, 0.3 us)
Async XLA Ops:
  0.0 32.8 %copy-start = (f32[128,1024]{1,0:T(8,128)S(1)}, f32[128,1024]{1,0:T(8,128)}, u32[]{:S(2)}) copy-start(f32[128,1024]{1,0:T(8,128)} %param.15) | copy-start | bytes 1572868
  1.7 35.1 %collective-permute-start.4 = (f32[1,32,1024]{2,1,0:T(8,128)S(1)}, f32[1,32,1024]{2,1,0:T(8,128)S(1)}, u32[]{:S(2)}, u32[]{:S(2)}) collective-permute-start(f32[1,32,1024]{2,1,0:T(8,128)S(1)} %get-tuple-element.23), channel_id=1, source_target_pairs={{2,0},{4,2},{6,4},{8,6},{10,8},{12,10},{14,12},{16,14},{18,16},{20... | collective-permute-start | bytes 393224 | tf_op jit(solution)/shard_map/ppermute | solution.py:18
  4.3 32.3 %collective-permute-start.5 = (f32[1,32,1024]{2,1,0:T(8,128)}, f32[1,32,1024]{2,1,0:T(8,128)S(1)}, u32[]{:S(2)}, u32[]{:S(2)}) collective-permute-start(f32[1,32,1024]{2,1,0:T(8,128)} %get-tuple-element.24), channel_id=1, source_target_pairs={{0,2},{2,4},{4,6},{6,8},{8,10},{10,12},{12,14},{14,16},{16,18},{18... | collective-permute-start | bytes 393224 | tf_op jit(solution)/shard_map/ppermute | solution.py:17
  8.9 13.2 %copy-start.7 = (s32[256,1]{0,1:T(1,128)S(1)}, s32[256,1]{0,1:T(1,128)}, u32[]{:S(2)}) copy-start(s32[256,1]{0,1:T(1,128)} %param.13) | copy-start | bytes 3076
  8.9 16.3 %copy-start.8 = (s32[256]{0:T(256)S(1)}, s32[256]{0:T(256)}, u32[]{:S(2)}) copy-start(s32[256]{0:T(256)} %param.14) | copy-start | bytes 3076
  8.9 19.3 %copy-start.6 = (f32[256,128]{1,0:T(8,128)S(1)}, f32[256,128]{1,0:T(8,128)}, u32[]{:S(2)}) copy-start(f32[256,128]{1,0:T(8,128)} %param.12) | copy-start | bytes 393220
  17.7 24.6 %collective-permute-start.1 = (f32[1,32,1024]{2,1,0:T(8,128)}, f32[1,32,1024]{2,1,0:T(8,128)S(1)}, u32[]{:S(2)}, u32[]{:S(2)}) collective-permute-start(f32[1,32,1024]{2,1,0:T(8,128)} %get-tuple-element.21), channel_id=1, source_target_pairs={{0,2},{2,4},{4,6},{6,8},{8,10},{10,12},{12,14},{14,16},{16,18},{18... | collective-permute-start | bytes 393224 | tf_op jit(solution)/shard_map/ppermute | solution.py:17
  20.1 22.2 %collective-permute-start = (f32[1,32,1024]{2,1,0:T(8,128)S(1)}, f32[1,32,1024]{2,1,0:T(8,128)S(1)}, u32[]{:S(2)}, u32[]{:S(2)}) collective-permute-start(f32[1,32,1024]{2,1,0:T(8,128)S(1)} %get-tuple-element.22), channel_id=1, source_target_pairs={{2,0},{4,2},{6,4},{8,6},{10,8},{12,10},{14,12},{16,14},{18,16},{20... | collective-permute-start | bytes 393224 | tf_op jit(solution)/shard_map/ppermute | solution.py:18
  34.6 2.0 %copy-start.1 = (f32[16,32,1024]{2,1,0:T(8,128)S(1)}, f32[16,32,1024]{2,1,0:T(8,128)}, u32[]{:S(2)}) copy-start(f32[16,32,1024]{2,1,0:T(8,128)} %param.8) | copy-start | bytes 6291460
  36.8 14.6 %copy-start.5 = (f32[18,32,1024]{2,1,0:T(8,128)}, f32[18,32,1024]{2,1,0:T(8,128)S(1)}, u32[]{:S(2)}) copy-start(f32[18,32,1024]{2,1,0:T(8,128)S(1)} %constant_dynamic-update-slice_fusion) | copy-start | bytes 7077892
  37.0 11.0 %collective-permute-start.6 = (f32[18,1,1024]{2,0,1:T(8,128)S(1)}, f32[18,1,1024]{2,0,1:T(8,128)S(1)}, u32[]{:S(2)}, u32[]{:S(2)}) collective-permute-start(f32[18,1,1024]{2,0,1:T(8,128)S(1)} %copy.35), channel_id=1, source_target_pairs={{1,0},{3,2},{5,4},{7,6},{9,8},{11,10},{13,12},{15,14},{17,16},{19,... | collective-permute-start | bytes 221192 | tf_op jit(solution)/shard_map/ppermute | solution.py:18
  38.3 9.8 %collective-permute-start.7 = (f32[18,1,1024]{2,0,1:T(8,128)S(1)}, f32[18,1,1024]{2,0,1:T(8,128)S(1)}, u32[]{:S(2)}, u32[]{:S(2)}) collective-permute-start(f32[18,1,1024]{2,0,1:T(8,128)S(1)} %copy.37), channel_id=1, source_target_pairs={{0,1},{2,3},{4,5},{6,7},{8,9},{10,11},{12,13},{14,15},{16,17},{18,... | collective-permute-start | bytes 221192 | tf_op jit(solution)/shard_map/ppermute | solution.py:17
  42.5 8.9 %collective-permute-start.2 = (f32[18,1,1024]{2,0,1:T(8,128)S(1)}, f32[18,1,1024]{2,0,1:T(8,128)S(1)}, u32[]{:S(2)}, u32[]{:S(2)}) collective-permute-start(f32[18,1,1024]{2,0,1:T(8,128)S(1)} %copy.29), channel_id=1, source_target_pairs={{1,0},{3,2},{5,4},{7,6},{9,8},{11,10},{13,12},{15,14},{17,16},{19,... | collective-permute-start | bytes 221192 | tf_op jit(solution)/shard_map/ppermute | solution.py:18
  43.8 7.7 %collective-permute-start.3 = (f32[18,1,1024]{2,0,1:T(8,128)S(1)}, f32[18,1,1024]{2,0,1:T(8,128)S(1)}, u32[]{:S(2)}, u32[]{:S(2)}) collective-permute-start(f32[18,1,1024]{2,0,1:T(8,128)S(1)} %copy.31), channel_id=1, source_target_pairs={{0,1},{2,3},{4,5},{6,7},{8,9},{10,11},{12,13},{14,15},{16,17},{18,... | collective-permute-start | bytes 221192 | tf_op jit(solution)/shard_map/ppermute | solution.py:17
  64.7 21.9 %copy-start.3 = (f32[16,32,1024]{2,1,0:T(8,128)}, f32[16,32,1024]{2,1,0:T(8,128)S(1)}, u32[]{:S(2)}) copy-start(f32[16,32,1024]{2,1,0:T(8,128)S(1)} %fusion.44) | copy-start | bytes 6291460
  64.7 10.4 %collective-permute-start.9 = (f32[1,32,1024]{2,1,0:T(8,128)S(1)}, f32[1,32,1024]{2,1,0:T(8,128)S(1)}, u32[]{:S(2)}, u32[]{:S(2)}) collective-permute-start(f32[1,32,1024]{2,1,0:T(8,128)S(1)} %get-tuple-element.19), channel_id=1, source_target_pairs={{0,2},{2,4},{4,6},{6,8},{8,10},{10,12},{12,14},{14,16},{16,18},{18... | collective-permute-start | bytes 393224 | tf_op jit(solution)/shard_map/ppermute | solution.py:17
  73.2 6.3 %collective-permute-start.8 = (f32[1,32,1024]{2,1,0:T(8,128)S(1)}, f32[1,32,1024]{2,1,0:T(8,128)S(1)}, u32[]{:S(2)}, u32[]{:S(2)}) collective-permute-start(f32[1,32,1024]{2,1,0:T(8,128)S(1)} %get-tuple-element.20), channel_id=1, source_target_pairs={{2,0},{4,2},{6,4},{8,6},{10,8},{12,10},{14,12},{16,14},{18,16},{20... | collective-permute-start | bytes 393224 | tf_op jit(solution)/shard_map/ppermute | solution.py:18
  79.6 5.4 %collective-permute-start.10 = (f32[18,1,1024]{2,0,1:T(8,128)S(1)}, f32[18,1,1024]{2,0,1:T(8,128)S(1)}, u32[]{:S(2)}, u32[]{:S(2)}) collective-permute-start(f32[18,1,1024]{2,0,1:T(8,128)S(1)} %copy.41), channel_id=1, source_target_pairs={{1,0},{3,2},{5,4},{7,6},{9,8},{11,10},{13,12},{15,14},{17,16},{19,... | collective-permute-start | bytes 221192 | tf_op jit(solution)/shard_map/ppermute | solution.py:18
  80.9 5.6 %collective-permute-start.11 = (f32[18,1,1024]{2,0,1:T(8,128)S(1)}, f32[18,1,1024]{2,0,1:T(8,128)S(1)}, u32[]{:S(2)}, u32[]{:S(2)}) collective-permute-start(f32[18,1,1024]{2,0,1:T(8,128)S(1)} %copy.43), channel_id=1, source_target_pairs={{0,1},{2,3},{4,5},{6,7},{8,9},{10,11},{12,13},{14,15},{16,17},{18,... | collective-permute-start | bytes 221192 | tf_op jit(solution)/shard_map/ppermute | solution.py:17
  103.0 19.5 %copy-start.4 = (f32[16,32,1024]{2,1,0:T(8,128)S(1)}, f32[16,32,1024]{2,1,0:T(8,128)}, u32[]{:S(2)}) copy-start(f32[16,32,1024]{2,1,0:T(8,128)} %fusion.31) | copy-start | bytes 6291460
  104.2 5.6 %collective-permute-start.13 = (f32[1,32,1024]{2,1,0:T(8,128)S(1)}, f32[1,32,1024]{2,1,0:T(8,128)S(1)}, u32[]{:S(2)}, u32[]{:S(2)}) collective-permute-start(f32[1,32,1024]{2,1,0:T(8,128)S(1)} %get-tuple-element.17), channel_id=1, source_target_pairs={{0,2},{2,4},{4,6},{6,8},{8,10},{10,12},{12,14},{14,16},{16,18},{18... | collective-permute-start | bytes 393224 | tf_op jit(solution)/shard_map/ppermute | solution.py:17
  107.1 7.1 %collective-permute-start.12 = (f32[1,32,1024]{2,1,0:T(8,128)S(1)}, f32[1,32,1024]{2,1,0:T(8,128)S(1)}, u32[]{:S(2)}, u32[]{:S(2)}) collective-permute-start(f32[1,32,1024]{2,1,0:T(8,128)S(1)} %get-tuple-element.18), channel_id=1, source_target_pairs={{2,0},{4,2},{6,4},{8,6},{10,8},{12,10},{14,12},{16,14},{18,16},{20... | collective-permute-start | bytes 393224 | tf_op jit(solution)/shard_map/ppermute | solution.py:18
  115.5 5.5 %collective-permute-start.14 = (f32[18,1,1024]{2,0,1:T(8,128)S(1)}, f32[18,1,1024]{2,0,1:T(8,128)S(1)}, u32[]{:S(2)}, u32[]{:S(2)}) collective-permute-start(f32[18,1,1024]{2,0,1:T(8,128)S(1)} %copy.47), channel_id=1, source_target_pairs={{1,0},{3,2},{5,4},{7,6},{9,8},{11,10},{13,12},{15,14},{17,16},{19,... | collective-permute-start | bytes 221192 | tf_op jit(solution)/shard_map/ppermute | solution.py:18
  116.9 5.6 %collective-permute-start.15 = (f32[18,1,1024]{2,0,1:T(8,128)S(1)}, f32[18,1,1024]{2,0,1:T(8,128)S(1)}, u32[]{:S(2)}, u32[]{:S(2)}) collective-permute-start(f32[18,1,1024]{2,0,1:T(8,128)S(1)} %copy.49), channel_id=1, source_target_pairs={{0,1},{2,3},{4,5},{6,7},{8,9},{10,11},{12,13},{14,15},{16,17},{18,... | collective-permute-start | bytes 221192 | tf_op jit(solution)/shard_map/ppermute | solution.py:17
  138.4 19.7 %copy-start.2 = (f32[16,32,1024]{2,1,0:T(8,128)S(1)}, f32[16,32,1024]{2,1,0:T(8,128)}, u32[]{:S(2)}) copy-start(f32[16,32,1024]{2,1,0:T(8,128)} %fusion.18) | copy-start | bytes 6291460
  139.6 5.7 %collective-permute-start.17 = (f32[1,32,1024]{2,1,0:T(8,128)S(1)}, f32[1,32,1024]{2,1,0:T(8,128)S(1)}, u32[]{:S(2)}, u32[]{:S(2)}) collective-permute-start(f32[1,32,1024]{2,1,0:T(8,128)S(1)} %get-tuple-element.15), channel_id=1, source_target_pairs={{0,2},{2,4},{4,6},{6,8},{8,10},{10,12},{12,14},{14,16},{16,18},{18... | collective-permute-start | bytes 393224 | tf_op jit(solution)/shard_map/ppermute | solution.py:17
  142.5 7.2 %collective-permute-start.16 = (f32[1,32,1024]{2,1,0:T(8,128)S(1)}, f32[1,32,1024]{2,1,0:T(8,128)S(1)}, u32[]{:S(2)}, u32[]{:S(2)}) collective-permute-start(f32[1,32,1024]{2,1,0:T(8,128)S(1)} %get-tuple-element.16), channel_id=1, source_target_pairs={{2,0},{4,2},{6,4},{8,6},{10,8},{12,10},{14,12},{16,14},{18,16},{20... | collective-permute-start | bytes 393224 | tf_op jit(solution)/shard_map/ppermute | solution.py:18
  151.1 5.4 %collective-permute-start.18 = (f32[18,1,1024]{2,0,1:T(8,128)S(1)}, f32[18,1,1024]{2,0,1:T(8,128)S(1)}, u32[]{:S(2)}, u32[]{:S(2)}) collective-permute-start(f32[18,1,1024]{2,0,1:T(8,128)S(1)} %copy.53), channel_id=1, source_target_pairs={{1,0},{3,2},{5,4},{7,6},{9,8},{11,10},{13,12},{15,14},{17,16},{19,... | collective-permute-start | bytes 221192 | tf_op jit(solution)/shard_map/ppermute | solution.py:18
  152.4 5.6 %collective-permute-start.19 = (f32[18,1,1024]{2,0,1:T(8,128)S(1)}, f32[18,1,1024]{2,0,1:T(8,128)S(1)}, u32[]{:S(2)}, u32[]{:S(2)}) collective-permute-start(f32[18,1,1024]{2,0,1:T(8,128)S(1)} %copy.55), channel_id=1, source_target_pairs={{0,1},{2,3},{4,5},{6,7},{8,9},{10,11},{12,13},{14,15},{16,17},{18,... | collective-permute-start | bytes 221192 | tf_op jit(solution)/shard_map/ppermute | solution.py:17
where the time goes:
time: 177 us; the launch traced here: 174 us
  other arithmetic  75.4 us (43%)
  starting transfers between devices  58.4 us (33%)
  waiting for transfers between devices  17.5 us (10%)
  blocking collectives  10.6 us (6%)
  local copies, waits for them, and re-layouts  7.52 us (4%)
  matrix products  3.8 us (2%)
    add x4, other arithmetic, shards(): temp = temp + 0.8 * (rhs - diag * temp + nbsum) / diag  44.8 us
    ppermute x10, starting transfers between devices, extended(): before = lax.ppermute(last, axis, up)  40.1 us
    concatenate x9, other arithmetic, extended(): x = jnp.concatenate([before, x, after], axis=dim)  22.4 us
    ppermute x10, starting transfers between devices, extended(): after = lax.ppermute(first, axis, down)  18.4 us
    ppermute x10, waiting for transfers between devices, extended(): after = lax.ppermute(first, axis, down)  13.2 us
    add x1, other arithmetic, shards(): cond + jnp.where(soil_class == klass, cond_table[klass], jnp.float32(0.0))  8.12 us
    all_gather x1, blocking collectives, shards(): lax.all_gather(losses, 'gy', axis=0, tiled=True)  4.48 us
    ppermute x10, waiting for transfers between devices, extended(): before = lax.ppermute(last, axis, up)  4.32 us
  transfers between devices with their start and end apart: 20, of which 6 were waited for; matrix products, arithmetic and copies ran while one was open for 11% of the time, Pallas kernels for 0%

commit v1 on v0

v1 whole, which is shorter than its diff:
```python
import functools

import jax
import jax.numpy as jnp
from jax import lax
from jax.experimental import pallas as pl
from jax.experimental.pallas import tpu as pltpu
from jax.sharding import PartitionSpec as P

SWEEPS = 4
F32 = jnp.float32
BF16 = jnp.bfloat16
MESH = pl.DeviceIdType.MESH


def split(x):
    hi = x.astype(BF16)
    return hi, (x - hi.astype(F32)).astype(BF16)


def kernel(
    n_gx, n_gy, t_hbm, cap_hbm, cls_hbm, table, loss_hbm, own_hbm, col_hbm, inj_hbm, out_hbm,
    t0, t1, cap, cls, inj, loss, own, col, cond, gx, gy, gz, half_w, base, source,
    halo_x, halo_y, cls_x, cls_y, stage_y, stage_cls, edge_y, chalo_y,
    load_sem, out_sem, xsend, xrecv, ysend, yrecv, lsend, lrecv,
):
    cx, cy, nz = cap.shape
    ncls = table.shape[0]
    me_x, me_y = lax.axis_index("gx"), lax.axis_index("gy")
    has = ((me_x > 0, me_x < n_gx - 1), (me_y > 0, me_y < n_gy - 1))
    other = ((me_x - 1, me_x + 1), (me_y - 1, me_y + 1))
    bufs = (t0, t1)

    loads = [
        pltpu.make_async_copy(src, dst, load_sem.at[n])
        for n, (src, dst) in enumerate((
            (t_hbm, t0), (cls_hbm, cls), (cap_hbm, cap), (loss_hbm, loss.at[0]),
            (own_hbm, own.at[0]), (col_hbm, col.at[0]), (inj_hbm, inj),
        ))
    ]
    for copy in loads:
        copy.start()

    barrier = pltpu.get_barrier_semaphore()
    for side in range(2):
        @pl.when(has[0][side])
        def _():
            pl.semaphore_signal(barrier, inc=1, device_id=(other[0][side], me_y), device_id_type=MESH)
    partners = [lax.rem(me_y + d, n_gy) for d in range(1, n_gy)]
    for partner in partners:
        pl.semaphore_signal(barrier, inc=1, device_id=(me_x, partner), device_id_type=MESH)
    pl.semaphore_wait(barrier, n_gy - 1 + jnp.where(has[0][0], 1, 0) + jnp.where(has[0][1], 1, 0))

    def remote(src, dst, send, recv, axis, side):
        target = (other[0][side], me_y) if axis == 0 else (me_x, other[1][side])
        return pltpu.make_async_remote_copy(
            src_ref=src, dst_ref=dst, send_sem=send, recv_sem=recv, device_id=target, device_id_type=MESH
        )

    def x_copy(k, side, src):
        dst = cls_x.at[1 - side] if k == SWEEPS else halo_x.at[k, 1 - side]
        return remote(src, dst, xsend.at[k, side], xrecv.at[k, 1 - side], 0, side)

    def y_copy(k, side):
        src, dst = (stage_cls.at[side], cls_y.at[1 - side]) if k == SWEEPS else (stage_y.at[k, side], halo_y.at[k, 1 - side])
        return remote(src, dst, ysend.at[k, side], yrecv.at[k, 1 - side], 1, side)

    def x_plane(k, side):
        plane = (0, cx - 1)[side]
        if k == SWEEPS:
            return cls_hbm.at[plane]
        return t_hbm.at[plane] if k == 0 else bufs[k % 2].at[plane]

    def send_x(k):
        for side in range(2):
            @pl.when(has[0][side])
            def _():
                x_copy(k, side, x_plane(k, side)).start()

    def send_y(k):
        for side in range(2):
            @pl.when(has[1][side])
            def _():
                y_copy(k, side).start()

    def await_x(k):
        for side in range(2):
            @pl.when(has[0][side])
            def _():
                x_copy(k, 1 - side, x_plane(k, 1 - side)).wait_recv()

    def await_y(k):
        for side in range(2):
            @pl.when(has[1][side])
            def _():
                y_copy(k, 1 - side).wait_recv()

    def sent_x(k):
        for side in range(2):
            @pl.when(has[0][side])
            def _():
                x_copy(k, side, x_plane(k, side)).wait_send()

    def sent_y(k):
        for side in range(2):
            @pl.when(has[1][side])
            def _():
                y_copy(k, side).wait_send()

    send_x(SWEEPS)
    send_x(0)
    loss_copies = [
        pltpu.make_async_remote_copy(
            src_ref=src, dst_ref=dst.at[d], send_sem=lsend.at[n, d], recv_sem=lrecv.at[n, d],
            device_id=(me_x, partners[d - 1]), device_id_type=MESH,
        )
        for d in range(1, n_gy)
        for n, (src, dst) in enumerate(((loss_hbm, loss), (own_hbm, own), (col_hbm, col)))
    ]
    for copy in loss_copies:
        copy.start()

    for axis, halos, ids in ((0, halo_x, cls_x), (1, halo_y, cls_y)):
        for side in range(2):
            @pl.when(jnp.logical_not(has[axis][side]))
            def _():
                ids[side] = jnp.zeros(ids.shape[1:], jnp.int32)
                for k in range(SWEEPS):
                    halos[k, side] = jnp.zeros(halos.shape[2:], F32)

    loads[1].wait()
    for side in range(2):
        stage_cls[side] = cls[:, (0, cy - 1)[side], :]
    send_y(SWEEPS)
    loads[0].wait()
    for side in range(2):
        stage_y[0, side] = t0[:, (0, cy - 1)[side], :]
    send_y(0)

    def look_up(ids):
        values = jnp.full(ids.shape, table[0], F32)
        for klass in range(1, ncls):
            values = jnp.where(ids == klass, table[klass], values)
        return values

    @pl.loop(0, cx)
    def _(i):
        cond[i + 1] = look_up(cls[i])

    for copy in loads[2:]:
        copy.wait()
    inj_hi, inj_lo = split(inj[...])
    inj_hi = jnp.concatenate([inj_hi, inj_hi], axis=0)
    inj_lo = jnp.concatenate([inj_lo, inj_lo], axis=0)
    for copy in loss_copies:
        copy.wait_recv()
    lw = loss.shape[2]
    spread = None
    for d in range(n_gy):
        hit = jnp.where(own[d] == me_y, col[d], -1)
        picker = hit == lax.broadcasted_iota(jnp.int32, (cx * cy, hit.shape[1]), 0)
        picker = jnp.where(picker, F32(1.0), F32(0.0)).astype(BF16)
        part = jnp.dot(picker, jnp.concatenate(split(loss[d]), axis=1), preferred_element_type=F32)
        spread = part if spread is None else spread + part
    spread = jnp.concatenate(split(spread[:, :lw] + spread[:, lw:]), axis=1)
    source[...] = jnp.dot(spread, inj_hi, preferred_element_type=F32) + jnp.dot(spread, inj_lo, preferred_element_type=F32)

    await_x(SWEEPS)
    for side in range(2):
        cond[(0, cx + 1)[side]] = look_up(cls_x[side]) * jnp.where(has[0][side], F32(1.0), F32(0.0))
    await_y(SWEEPS)
    for side in range(2):
        chalo_y[side] = look_up(cls_y[side]) * jnp.where(has[1][side], F32(1.0), F32(0.0))

    gx[cx] = cond[cx] + cond[cx + 1]

    @pl.loop(0, cx)
    def _(i):
        row = lax.broadcasted_iota(jnp.int32, (cy, nz), 0)
        lane = lax.broadcasted_iota(jnp.int32, (cy, nz), 1)
        low, here, high = cond[i], cond[i + 1], cond[i + 2]
        gx[i] = low + here
        y_low, y_high = chalo_y[0, pl.ds(i, 1), :], chalo_y[1, pl.ds(i, 1), :]
        after = pltpu.roll(here, cy - 1, 0)
        gy[i] = jnp.where(row == cy - 1, F32(0.0), here + after)
        total = low + high + jnp.where(row == cy - 1, y_high, after)
        total = total + jnp.where(row == 0, y_low, pltpu.roll(here, 1, 0))
        after = jnp.where(lane == nz - 1, F32(0.0), pltpu.roll(here, nz - 1, 1))
        gz[i] = jnp.where(lane == nz - 1, F32(0.0), here + after)
        total = total + after + jnp.where(lane == 0, F32(0.0), pltpu.roll(here, 1, 1))
        weight = 0.4 / (cap[i] + (3.0 * here + 0.5 * total))
        half_w[i] = weight
        base[i] = 2.0 * weight * (cap[i] * t0[i] + source[pl.ds(pl.multiple_of(i * cy, cy), cy), :])
        edge_y[0, pl.ds(i, 1), :] = weight[:1] * (here[:1] + y_low)
        edge_y[1, pl.ds(i, 1), :] = weight[cy - 1:] * (here[cy - 1:] + y_high)

    def advance(now, new, i, low, high):
        here = now[i]
        total = gx[i] * low + gx[i + 1] * high
        face = gy[i]
        total = total + face * pltpu.roll(here, cy - 1, 0) + pltpu.roll(face * here, 1, 0)
        face = gz[i]
        total = total + face * pltpu.roll(here, nz - 1, 1) + pltpu.roll(face * here, 1, 1)
        new[i] = 0.2 * here + base[i] + half_w[i] * total

    for k in range(SWEEPS):
        now, new = bufs[k % 2], bufs[(k + 1) % 2]

        @pl.loop(1, cx - 1)
        def _(i):
            advance(now, new, i, now[i - 1], now[i + 1])

        if k >= 2:
            sent_x(k - 1)
        await_x(k)
        advance(now, new, 0, halo_x[k, 0], now[1])
        advance(now, new, cx - 1, now[cx - 2], halo_x[k, 1])
        await_y(k)
        for side in range(2):
            spot = (0, cy - 1)[side]
            fixed = new[:, spot, :] + edge_y[side] * halo_y[k, side]
            new[:, spot, :] = fixed
            if k + 1 < SWEEPS:
                stage_y[k + 1, side] = fixed
        if k + 1 < SWEEPS:
            send_x(k + 1)
            send_y(k + 1)

    done = pltpu.make_async_copy(bufs[SWEEPS % 2], out_hbm, out_sem)
    done.start()
    sent_x(SWEEPS)
    sent_x(0)
    sent_x(SWEEPS - 1)
    for k in range(SWEEPS + 1):
        sent_y(k)
    for copy in loss_copies:
        copy.wait_send()
    done.wait()


def solution(mesh):
    n_gx, n_gy = mesh.shape["gx"], mesh.shape["gy"]

    def shards(temp_old, capacity, soil_class, cond_table, losses, owner, column, injection):
        cx, cy, nz = temp_old.shape
        segments, lw = losses.shape
        owner, column = owner.reshape(1, segments), column.reshape(1, segments)
        field = pltpu.VMEM((cx, cy, nz), F32)
        any_spec = pl.BlockSpec(memory_space=pl.ANY)
        dma = pltpu.SemaphoreType.DMA
        return pl.pallas_call(
            functools.partial(kernel, n_gx, n_gy),
            out_shape=jax.ShapeDtypeStruct(temp_old.shape, F32),
            in_specs=[any_spec] * 3 + [pl.BlockSpec(memory_space=pltpu.SMEM)] + [any_spec] * 4,
            out_specs=any_spec,
            scratch_shapes=[
                field, field, field,
                pltpu.VMEM((cx, cy, nz), jnp.int32),
                pltpu.VMEM(injection.shape, F32),
                pltpu.VMEM((n_gy, segments, lw), F32),
                pltpu.VMEM((n_gy, 1, segments), jnp.int32),
                pltpu.VMEM((n_gy, 1, segments), jnp.int32),
                pltpu.VMEM((cx + 2, cy, nz), F32),
                pltpu.VMEM((cx + 1, cy, nz), F32),
                field, field, field, field,
                pltpu.VMEM((cx * cy, nz), F32),
                pltpu.VMEM((SWEEPS, 2, cy, nz), F32),
                pltpu.VMEM((SWEEPS, 2, cx, nz), F32),
                pltpu.VMEM((2, cy, nz), jnp.int32),
                pltpu.VMEM((2, cx, nz), jnp.int32),
                pltpu.VMEM((SWEEPS, 2, cx, nz), F32),
                pltpu.VMEM((2, cx, nz), jnp.int32),
                pltpu.VMEM((2, cx, nz), F32),
                pltpu.VMEM((2, cx, nz), F32),
                dma((7,)), dma(()),
                dma((SWEEPS + 1, 2)), dma((SWEEPS + 1, 2)), dma((SWEEPS + 1, 2)), dma((SWEEPS + 1, 2)),
                dma((3, n_gy)), dma((3, n_gy)),
            ],
            compiler_params=pltpu.CompilerParams(
                collective_id=0, has_side_effects=True, vmem_limit_bytes=60 * 2**20
            ),
        )(temp_old, capacity, soil_class, cond_table, losses, owner, column, injection)

    return jax.shard_map(
        shards,
        mesh=mesh,
        in_specs=(
            P("gx", "gy", None),
            P("gx", "gy", None),
            P("gx", "gy", None),
            P(),
            P(("gx", "gy"), None),
            P(("gx", "gy"), None),
            P(("gx", "gy")),
            P(),
        ),
        out_specs=P("gx", "gy", None),
        check_vma=False,
    )
```

time: 177 us -> 34.4 us (0.19); the launches traced: 174 us -> 34.2 us
  other arithmetic: 75.4 us -> 0 us
  starting transfers between devices: 58.4 us -> 0 us
  Pallas kernels: 0 us -> 31.1 us
  waiting for transfers between devices: 17.5 us -> 0 us
  blocking collectives: 10.6 us -> 0 us
  local copies, waits for them, and re-layouts: 7.52 us -> 3.16 us
  matrix products: 3.8 us -> 0 us
    ppermute x20 -> x0, starting transfers between devices: 58.4 us -> none  [the longest x10 40.1 us: extended(): before = lax.ppermute(last, axis, up)]
    add x5 -> x0, other arithmetic: 52.9 us -> none  [the longest x4 44.8 us: shards(): temp = temp + 0.8 * (rhs - diag * temp + nbsum) / diag]
    pallas_call x0 -> x1, Pallas kernels: none -> 31.1 us  [shards(): pl.pallas_call(functools.partial(kernel, n_gx, n_gy), out_shape=jax.Shape...]
    concatenate x9 -> x0, other arithmetic: 22.4 us -> none  [extended(): x = jnp.concatenate([before, x, after], axis=dim)]
    ppermute x20 -> x0, waiting for transfers between devices: 17.5 us -> none  [the longest x10 13.2 us: extended(): after = lax.ppermute(first, axis, down)]
    all_gather x3 -> x0, blocking collectives: 10.6 us -> none  [the longest x1 4.48 us: shards(): lax.all_gather(losses, 'gy', axis=0, tiled=True)]
    slice x17 -> x0, local copies, waits for them, and re-layouts: 6.54 us -> none  [the longest x10 3.16 us: extended(): last = lax.slice_in_dim(x, length - width, length, axis=dim)]
    dot_general x2 -> x0, matrix products: 3.8 us -> none  [the longest x1 2 us: shards(): jnp.dot(picker, profile, precision=lax.Precision.HIGHEST, preferred_eleme...]
  transfers between devices with their start and end apart: 20 -> 0, of which waited for: 6 -> 0; matrix products, arithmetic and copies ran while one was open for 11% -> 0% of each run, Pallas kernels for 0% -> 0%
where the time goes in v1:
time: 34.4 us; the launch traced here: 34.2 us
  Pallas kernels  31.1 us (90%)
  local copies, waits for them, and re-layouts  3.16 us (9%)
    pallas_call x1, Pallas kernels, shards(): pl.pallas_call(functools.partial(kernel, n_gx, n_gy), out_shape=jax.Shape...  31.1 us
    unnamed x1, local copies, waits for them, and re-layouts  3.16 us

profile of v1, /device:TPU:9, one launch (start us, length us, event | category | flops | bytes accessed | tf_op | source)
XLA Modules:
  0.0 34.2 jit_solution(11862158891858419100)
XLA Ops:
  0.0 31.1 %shard_map.82 = f32[16,32,1024]{2,1,0:T(8,128)} custom-call(f32[16,32,1024]{2,1,0:T(8,128)} %t_hbm.1, f32[16,32,1024]{2,1,0:T(8,128)} %cap_hbm.1, s32[16,32,1024]{2,1,0:T(8,128)} %cls_hbm.1, f32[8]{0:T(128)} %table.1, f32[256,128]{1,0:T(8,128)} %loss_hbm.1, s32[1,256]{1,0:T(1,128)} %bitcast.2, s32[1,256]{1,0:T(1,128)} %bitcast.3, f32[128,1024]{1,0:T(8,128)} %inj_hbm.1), custom_call_target="tpu_custom_call" | custom-call | tf_op jit(solution)/shard_map/pallas_call | solution.py:251
  31.1 3.2 %copy.10 = f32[16,32,1024]{2,1,0:T(8,128)} copy(f32[16,32,1024]{2,1,0:T(8,128)} %shard_map.82) | data formatting | bytes 4194304

commit v2 on v1

--- a/solution.py
+++ b/solution.py
@@ -8,6 +8,7 @@
 from jax.sharding import PartitionSpec as P
 
 SWEEPS = 4
+VMEM_LIMIT = 64_946_176
 F32 = jnp.float32
 BF16 = jnp.bfloat16
 MESH = pl.DeviceIdType.MESH
@@ -19,17 +20,17 @@
 
 
 def kernel(
-    n_gx, n_gy, t_hbm, cap_hbm, cls_hbm, table, loss_hbm, own_hbm, col_hbm, inj_hbm, out_hbm,
+    n_gx, n_gy, t_hbm, cap_hbm, cls_hbm, table, loss_hbm, own_hbm, col_hbm, inj_hbm, out,
     t0, t1, cap, cls, inj, loss, own, col, cond, gx, gy, gz, half_w, base, source,
     halo_x, halo_y, cls_x, cls_y, stage_y, stage_cls, edge_y, chalo_y,
-    load_sem, out_sem, xsend, xrecv, ysend, yrecv, lsend, lrecv,
+    load_sem, xsend, xrecv, ysend, yrecv, lsend, lrecv,
 ):
     cx, cy, nz = cap.shape
     ncls = table.shape[0]
     me_x, me_y = lax.axis_index("gx"), lax.axis_index("gy")
     has = ((me_x > 0, me_x < n_gx - 1), (me_y > 0, me_y < n_gy - 1))
     other = ((me_x - 1, me_x + 1), (me_y - 1, me_y + 1))
-    bufs = (t0, t1)
+    bufs = [(t0, t1)[k % 2] for k in range(SWEEPS)] + [out]
 
     loads = [
         pltpu.make_async_copy(src, dst, load_sem.at[n])
@@ -69,7 +70,7 @@
         plane = (0, cx - 1)[side]
         if k == SWEEPS:
             return cls_hbm.at[plane]
-        return t_hbm.at[plane] if k == 0 else bufs[k % 2].at[plane]
+        return t_hbm.at[plane] if k == 0 else bufs[k].at[plane]
 
     def send_x(k):
         for side in range(2):
@@ -117,8 +118,17 @@
         for d in range(1, n_gy)
         for n, (src, dst) in enumerate(((loss_hbm, loss), (own_hbm, own), (col_hbm, col)))
     ]
+
+    loads[1].wait()
+    for side in range(2):
+        stage_cls[side] = cls[:, (0, cy - 1)[side], :]
+    send_y(SWEEPS)
     for copy in loss_copies:
         copy.start()
+    loads[0].wait()
+    for side in range(2):
+        stage_y[0, side] = t0[:, (0, cy - 1)[side], :]
+    send_y(0)
 
     for axis, halos, ids in ((0, halo_x, cls_x), (1, halo_y, cls_y)):
         for side in range(2):
@@ -127,15 +137,6 @@
                 ids[side] = jnp.zeros(ids.shape[1:], jnp.int32)
                 for k in range(SWEEPS):
                     halos[k, side] = jnp.zeros(halos.shape[2:], F32)
-
-    loads[1].wait()
-    for side in range(2):
-        stage_cls[side] = cls[:, (0, cy - 1)[side], :]
-    send_y(SWEEPS)
-    loads[0].wait()
-    for side in range(2):
-        stage_y[0, side] = t0[:, (0, cy - 1)[side], :]
-    send_y(0)
 
     def look_up(ids):
         values = jnp.full(ids.shape, table[0], F32)
@@ -147,7 +148,34 @@
     def _(i):
         cond[i + 1] = look_up(cls[i])
 
-    for copy in loads[2:]:
+    await_y(SWEEPS)
+    for side in range(2):
+        chalo_y[side] = look_up(cls_y[side]) * jnp.where(has[1][side], F32(1.0), F32(0.0))
+    loads[2].wait()
+
+    def prepare(i):
+        row = lax.broadcasted_iota(jnp.int32, (cy, nz), 0)
+        lane = lax.broadcasted_iota(jnp.int32, (cy, nz), 1)
+        low, here, high = cond[i], cond[i + 1], cond[i + 2]
+        gx[i] = low + here
+        y_low, y_high = chalo_y[0, pl.ds(i, 1), :], chalo_y[1, pl.ds(i, 1), :]
+        after = pltpu.roll(here, cy - 1, 0)
+        gy[i] = jnp.where(row == cy - 1, F32(0.0), here + after)
+        total = low + high + jnp.where(row == cy - 1, y_high, after)
+        total = total + jnp.where(row == 0, y_low, pltpu.roll(here, 1, 0))
+        after = jnp.where(lane == nz - 1, F32(0.0), pltpu.roll(here, nz - 1, 1))
+        gz[i] = jnp.where(lane == nz - 1, F32(0.0), here + after)
+        total = total + after + jnp.where(lane == 0, F32(0.0), pltpu.roll(here, 1, 1))
+        weight = 0.4 / (cap[i] + (3.0 * here + 0.5 * total))
+        half_w[i] = weight
+        edge_y[0, pl.ds(i, 1), :] = weight[:1] * (here[:1] + y_low)
+        edge_y[1, pl.ds(i, 1), :] = weight[cy - 1:] * (here[cy - 1:] + y_high)
+
+    @pl.loop(1, cx - 1)
+    def _(i):
+        prepare(i)
+
+    for copy in loads[3:]:
         copy.wait()
     inj_hi, inj_lo = split(inj[...])
     inj_hi = jnp.concatenate([inj_hi, inj_hi], axis=0)
@@ -168,74 +196,80 @@
     await_x(SWEEPS)
     for side in range(2):
         cond[(0, cx + 1)[side]] = look_up(cls_x[side]) * jnp.where(has[0][side], F32(1.0), F32(0.0))
-    await_y(SWEEPS)
-    for side in range(2):
-        chalo_y[side] = look_up(cls_y[side]) * jnp.where(has[1][side], F32(1.0), F32(0.0))
-
+    prepare(0)
+    prepare(cx - 1)
     gx[cx] = cond[cx] + cond[cx + 1]
 
-    @pl.loop(0, cx)
-    def _(i):
-        row = lax.broadcasted_iota(jnp.int32, (cy, nz), 0)
-        lane = lax.broadcasted_iota(jnp.int32, (cy, nz), 1)
-        low, here, high = cond[i], cond[i + 1], cond[i + 2]
-        gx[i] = low + here
-        y_low, y_high = chalo_y[0, pl.ds(i, 1), :], chalo_y[1, pl.ds(i, 1), :]
-        after = pltpu.roll(here, cy - 1, 0)
-        gy[i] = jnp.where(row == cy - 1, F32(0.0), here + after)
-        total = low + high + jnp.where(row == cy - 1, y_high, after)
-        total = total + jnp.where(row == 0, y_low, pltpu.roll(here, 1, 0))
-        after = jnp.where(lane == nz - 1, F32(0.0), pltpu.roll(here, nz - 1, 1))
-        gz[i] = jnp.where(lane == nz - 1, F32(0.0), here + after)
-        total = total + after + jnp.where(lane == 0, F32(0.0), pltpu.roll(here, 1, 1))
-        weight = 0.4 / (cap[i] + (3.0 * here + 0.5 * total))
-        half_w[i] = weight
-        base[i] = 2.0 * weight * (cap[i] * t0[i] + source[pl.ds(pl.multiple_of(i * cy, cy), cy), :])
-        edge_y[0, pl.ds(i, 1), :] = weight[:1] * (here[:1] + y_low)
-        edge_y[1, pl.ds(i, 1), :] = weight[cy - 1:] * (here[cy - 1:] + y_high)
-
-    def advance(now, new, i, low, high):
-        here = now[i]
+    def advance(k, i, low, high):
+        here = bufs[k][i]
+        weight = half_w[i]
         total = gx[i] * low + gx[i + 1] * high
         face = gy[i]
         total = total + face * pltpu.roll(here, cy - 1, 0) + pltpu.roll(face * here, 1, 0)
         face = gz[i]
         total = total + face * pltpu.roll(here, nz - 1, 1) + pltpu.roll(face * here, 1, 1)
-        new[i] = 0.2 * here + base[i] + half_w[i] * total
-
-    for k in range(SWEEPS):
-        now, new = bufs[k % 2], bufs[(k + 1) % 2]
-
-        @pl.loop(1, cx - 1)
-        def _(i):
-            advance(now, new, i, now[i - 1], now[i + 1])
-
-        if k >= 2:
-            sent_x(k - 1)
-        await_x(k)
-        advance(now, new, 0, halo_x[k, 0], now[1])
-        advance(now, new, cx - 1, now[cx - 2], halo_x[k, 1])
-        await_y(k)
+        if k == 0:
+            start = i * cy if isinstance(i, int) else pl.multiple_of(i * cy, cy)
+            known = 2.0 * weight * (cap[i] * here + source[pl.ds(start, cy), :])
+            base[i] = known
+        else:
+            known = base[i]
+        bufs[k + 1][i] = 0.2 * here + known + weight * total
+
+    def fix_plane(k, i):
+        new = bufs[k + 1]
+        for side in range(2):
+            spot = (0, cy - 1)[side]
+            fixed = new[i, spot:spot + 1, :] + edge_y[side, pl.ds(i, 1), :] * halo_y[k, side, pl.ds(i, 1), :]
+            new[i, spot:spot + 1, :] = fixed
+            stage_y[k + 1, side, pl.ds(i, 1), :] = fixed
+
+    def fix_all(k):
+        new = bufs[k + 1]
         for side in range(2):
             spot = (0, cy - 1)[side]
             fixed = new[:, spot, :] + edge_y[side] * halo_y[k, side]
             new[:, spot, :] = fixed
             if k + 1 < SWEEPS:
                 stage_y[k + 1, side] = fixed
+
+    def edges(k):
+        await_x(k)
+        advance(k, 0, halo_x[k, 0], bufs[k][1])
+        advance(k, cx - 1, bufs[k][cx - 2], halo_x[k, 1])
+        await_y(k)
+
+    def middle(k, fix):
+        @pl.loop(1, cx - 1)
+        def _(i):
+            advance(k, i, bufs[k][i - 1], bufs[k][i + 1])
+            if fix:
+                fix_plane(k, i)
+
+    edges(0)
+    fix_plane(0, 0)
+    fix_plane(0, cx - 1)
+    send_x(1)
+    middle(0, True)
+    send_y(1)
+    for k in range(1, SWEEPS):
+        middle(k, False)
+        if 2 <= k < SWEEPS - 1:
+            sent_x(k - 1)
+        edges(k)
+        fix_all(k)
         if k + 1 < SWEEPS:
             send_x(k + 1)
             send_y(k + 1)
 
-    done = pltpu.make_async_copy(bufs[SWEEPS % 2], out_hbm, out_sem)
-    done.start()
     sent_x(SWEEPS)
     sent_x(0)
-    sent_x(SWEEPS - 1)
+    for k in range(max(1, SWEEPS - 2), SWEEPS):
+        sent_x(k)
     for k in range(SWEEPS + 1):
         sent_y(k)
     for copy in loss_copies:
         copy.wait_send()
-    done.wait()
 
 
 def solution(mesh):
@@ -246,13 +280,13 @@
         segments, lw = losses.shape
         owner, column = owner.reshape(1, segments), column.reshape(1, segments)
         field = pltpu.VMEM((cx, cy, nz), F32)
-        any_spec = pl.BlockSpec(memory_space=pl.ANY)
+        any_spec = pl.BlockSpec(memory_space=pltpu.HBM)
         dma = pltpu.SemaphoreType.DMA
         return pl.pallas_call(
             functools.partial(kernel, n_gx, n_gy),
-            out_shape=jax.ShapeDtypeStruct(temp_old.shape, F32),
+            out_shape=pltpu.VMEM(temp_old.shape, F32),
             in_specs=[any_spec] * 3 + [pl.BlockSpec(memory_space=pltpu.SMEM)] + [any_spec] * 4,
-            out_specs=any_spec,
+            out_specs=pl.BlockSpec(memory_space=pltpu.VMEM),
             scratch_shapes=[
                 field, field, field,
                 pltpu.VMEM((cx, cy, nz), jnp.int32),
@@ -272,12 +306,12 @@
                 pltpu.VMEM((2, cx, nz), jnp.int32),
                 pltpu.VMEM((2, cx, nz), F32),
                 pltpu.VMEM((2, cx, nz), F32),
-                dma((7,)), dma(()),
+                dma((7,)),
                 dma((SWEEPS + 1, 2)), dma((SWEEPS + 1, 2)), dma((SWEEPS + 1, 2)), dma((SWEEPS + 1, 2)),
                 dma((3, n_gy)), dma((3, n_gy)),
             ],
             compiler_params=pltpu.CompilerParams(
-                collective_id=0, has_side_effects=True, vmem_limit_bytes=60 * 2**20
+                collective_id=0, has_side_effects=True, vmem_limit_bytes=VMEM_LIMIT
             ),
         )(temp_old, capacity, soil_class, cond_table, losses, owner, column, injection)
 

time: 34.4 us -> 29.3 us (0.85)
  Pallas kernels: 31.1 us -> 27.8 us
  local copies, waits for them, and re-layouts: 3.16 us -> 1.32 us
    pallas_call x1, Pallas kernels: 31.1 us -> 27.8 us  [shards(): pl.pallas_call(functools.partial(kernel, n_gx, n_gy), out_shape=pltpu.VME...]
    unnamed x1, local copies, waits for them, and re-layouts: 3.16 us -> 1.32 us
where the time goes in v2:
time: 29.3 us; the launch traced here: 29.1 us
  Pallas kernels  27.8 us (95%)
  local copies, waits for them, and re-layouts  1.32 us (5%)
    pallas_call x1, Pallas kernels, shards(): pl.pallas_call(functools.partial(kernel, n_gx, n_gy), out_shape=pltpu.VME...  27.8 us
    unnamed x1, local copies, waits for them, and re-layouts  1.32 us

profile of v2, /device:TPU:9, one launch (start us, length us, event | category | flops | bytes accessed | tf_op | source)
XLA Modules:
  0.0 29.1 jit_solution(14187939722276711644)
XLA Ops:
  0.0 27.8 %shard_map.82 = f32[16,32,1024]{2,1,0:T(8,128)S(1)} custom-call(f32[16,32,1024]{2,1,0:T(8,128)} %t_hbm.1, f32[16,32,1024]{2,1,0:T(8,128)} %cap_hbm.1, s32[16,32,1024]{2,1,0:T(8,128)} %cls_hbm.1, f32[8]{0:T(128)} %table.1, f32[256,128]{1,0:T(8,128)} %loss_hbm.1, s32[1,256]{1,0:T(1,128)} %bitcast.2, s32[1,256]{1,0:T(1,128)} %bitcast.3, f32[128,1024]{1,0:T(8,128)} %inj_hbm.1), custom_call_target="tpu_custom_call" | custom-call | tf_op jit(solution)/shard_map/pallas_call | solution.py:285
  27.8 1.3 %copy.10 = f32[16,32,1024]{2,1,0:T(8,128)} copy(f32[16,32,1024]{2,1,0:T(8,128)S(1)} %shard_map.82) | data formatting | bytes 4194304
